TPU v7x, 32 devices: a whole 2x2x4 slice. The times are simulated.
32 devices in a mesh: lat: 4 (over x, core), lon: 8 (over z, y).
Axes of the slice: x: 2, y: 2, z: 4, core: 2. Of those that a mesh axis runs over, the one named last changes fastest.
Arguments:
- node_latent: bfloat16 [64, 256, 512], P('lat', 'lon'), may hold values from -6 to 6
- edge_latent: bfloat16 [65536, 512], P(('lat', 'lon')), may hold values from -6 to 6
- sender: int32 [65536], P(('lat', 'lon')), may hold values from -1 to 16383, as said below
- receiver: int32 [65536], P(('lat', 'lon')), may hold values from -1 to 127, as said below
- block_tile: int32 [512], P(('lat', 'lon')), may hold values from 0 to 3, as said below
- w_first: bfloat16 [1536, 512], replicated, may hold values from -0.15625 to 0.15625
- w_second: bfloat16 [512, 512], replicated, may hold values from -0.25 to 0.25
- edge_gain: float32 [512], replicated, may hold values from 0.5 to 1.5
- w_node_first: bfloat16 [1024, 512], replicated, may hold values from -0.1875 to 0.1875
- w_node_second: bfloat16 [512, 512], replicated, may hold values from -0.25 to 0.25
- node_gain: float32 [512], replicated, may hold values from 0.5 to 1.5
Outputs:
- node_out: bfloat16 [64, 256, 512], P('lat', 'lon')
- edge_out: bfloat16 [65536, 512], P(('lat', 'lon'))
Inputs may be any that keep to these rules, and one draw needn't show every extreme that they name: `sender`: -1 on padded slots; otherwise the id of one of the eight grid neighbours of the edge's receiver node (columns wrap around, rows do not), or of a node whose row and column are both multiples of 4, anywhere on the grid. `receiver`: padded slots (-1) stand at the end of each block, at least 32 slots of a block are live, and live values never fall within a block. `block_tile`: never falls from one block of a device to the next, over the device's 16 blocks.
All inputs are finite; a program needn't handle non-finite values.
Results may differ from a plain program's by a relative error of at most 0.008.
Values may be sent and summed in bfloat16 or wider, within the bound.
A program may use at most 128 MiB of HBM per device.

v0:
```python
import jax
import jax.numpy as jnp
from jax import lax
from jax.sharding import PartitionSpec as P


def padded(value, sides, width, wrap):
    for axis, dim in sides:
        devices, length = (lax.axis_size(axis), value.shape[dim])
        up = [(i, (i + 1) % devices) for i in range(devices if wrap else devices - 1)]
        down = [(j, i) for i, j in up]
        last = lax.slice_in_dim(value, length - width, length, axis=dim)
        leading = lax.slice_in_dim(value, 0, width, axis=dim)
        before = lax.ppermute(last, axis, up)
        after = lax.ppermute(leading, axis, down)
        value = jnp.concatenate([before, value, after], axis=dim)
    return value


def layer_norm(values, gain_vec):
    average = jnp.mean(values, -1, keepdims=True)
    centred = values - average
    spread = jnp.mean(centred * centred, -1, keepdims=True)
    return centred * lax.rsqrt(spread + 1e-05) * gain_vec


def coarse_table(coarse_own):
    return lax.all_gather(coarse_own, ("lat", "lon"), axis=0, tiled=True)


def per_device(
    node_latent,
    edge_latent,
    sender,
    receiver,
    block_tile,
    w_first,
    w_second,
    edge_gain,
    w_node_first,
    w_node_second,
    node_gain,
):
    patch_rows, patch_cols, features = node_latent.shape
    lon_count = lax.axis_size("lon")
    lat_index = lax.axis_index("lat")
    lon_index = lax.axis_index("lon")
    grid_cols = patch_cols * lon_count
    blocks = block_tile.shape[0]
    block_len = edge_latent.shape[0] // blocks
    tile_nodes = 4 * patch_cols
    node_count = patch_rows * patch_cols
    own_rows = node_latent.reshape(node_count, features)
    coarse_own = node_latent[::4, ::4].reshape(-1, features)
    widened = padded(node_latent, (("lon", 1),), 1, True)
    extended = padded(widened, (("lat", 0),), 1, False)
    ext_rows = extended.reshape(-1, features)
    ext_count = ext_rows.shape[0]
    coarse_rows = coarse_table(coarse_own)
    lookup = jnp.concatenate([ext_rows, coarse_rows], axis=0)
    senders = jnp.maximum(sender, 0)
    send_row = senders // grid_cols
    send_col = senders % grid_cols
    near_row = send_row - lat_index * patch_rows + 1
    near_col = (send_col - lon_index * patch_cols + 1) % grid_cols
    is_near = (near_row >= 0) & (near_row <= patch_rows + 1) & (near_col <= patch_cols + 1)
    near_index = jnp.clip(near_row, 0, patch_rows + 1) * (patch_cols + 2) + jnp.clip(
        near_col, 0, patch_cols + 1
    )
    coarse_per = patch_rows // 4 * (patch_cols // 4)
    far_index = (
        (send_row // patch_rows * lon_count + send_col // patch_cols) * coarse_per
        + send_row % patch_rows // 4 * (patch_cols // 4)
        + send_col % patch_cols // 4
    )
    table_index = jnp.where(is_near, near_index, ext_count + far_index)
    live_slot = receiver >= 0
    tile_of = jnp.broadcast_to(block_tile[:, None], (blocks, block_len)).reshape(-1)
    local_index = jnp.where(live_slot, tile_of * tile_nodes + receiver, -1)
    recv_index = jnp.maximum(local_index, 0)
    w_edge = w_first[:features]
    w_send = w_first[features : 2 * features]
    w_recv = w_first[2 * features :]
    edge_proj = jnp.dot(edge_latent, w_edge, preferred_element_type=jnp.float32)
    send_rows = lookup[table_index]
    recv_rows = own_rows[recv_index]
    first_sum = (
        edge_proj
        + jnp.dot(send_rows, w_send, preferred_element_type=jnp.float32)
        + jnp.dot(recv_rows, w_recv, preferred_element_type=jnp.float32)
    )
    hidden = jax.nn.silu(first_sum).astype(jnp.bfloat16)
    second_sum = jnp.dot(hidden, w_second, preferred_element_type=jnp.float32)
    message = layer_norm(second_sum, edge_gain).astype(jnp.bfloat16)
    updated = jnp.where(
        live_slot[:, None], edge_latent.astype(jnp.float32) + message.astype(jnp.float32), 0.0
    ).astype(jnp.bfloat16)
    one_hot = (jnp.arange(node_count, dtype=jnp.int32)[:, None] == local_index[None, :]).astype(
        jnp.bfloat16
    )
    summed = jnp.dot(one_hot, message, preferred_element_type=jnp.float32)
    aggregate = summed.astype(jnp.bfloat16)
    node_first = jnp.dot(
        own_rows, w_node_first[:features], preferred_element_type=jnp.float32
    ) + jnp.dot(aggregate, w_node_first[features:], preferred_element_type=jnp.float32)
    node_hidden = jax.nn.silu(node_first).astype(jnp.bfloat16)
    node_second = jnp.dot(node_hidden, w_node_second, preferred_element_type=jnp.float32)
    node_out = (own_rows.astype(jnp.float32) + layer_norm(node_second, node_gain)).astype(
        jnp.bfloat16
    )
    return (node_out.reshape(patch_rows, patch_cols, features), updated)


def solution(mesh):
    return jax.shard_map(
        per_device,
        mesh=mesh,
        in_specs=(
            P("lat", "lon", None),
            P(("lat", "lon"), None),
            P(("lat", "lon")),
            P(("lat", "lon")),
            P(("lat", "lon")),
            P(),
            P(),
            P(),
            P(),
            P(),
            P(),
        ),
        out_specs=(P("lat", "lon", None), P(("lat", "lon"), None)),
        check_vma=False,
    )
```

profile of v0, /device:TPU:0, one launch (start us, length us, event | category | flops | bytes accessed | tf_op | source)
XLA Modules:
  0.0 116.1 jit_solution(6726447915008505783)
XLA Ops:
  7.2 0.0 copy-start
  7.2 0.0 copy-start.3
  7.2 0.0 all-gather.2.cloned.1.call-start
  7.2 3.2 %slice.36 = bf16[4,8,512]{2,1,0:T(8,128)(2,1)} slice(bf16[16,32,512]{2,1,0:T(8,128)(2,1)} %param.11), slice={[0:16:4], [0:32:4], [0:512:1]} | slice | bytes 65536 | tf_op jit(solution)/shard_map/slice | solution.py:54
  10.4 0.0 all-gather.2.cloned.1.call-update
  10.5 1.0 fusion.36
  11.5 3.0 %collective-permute-start = (bf16[16,1,512]{2,1,0:T(2,128)(2,1)S(1)}, bf16[16,1,512]{2,1,0:T(2,128)(2,1)S(1)}, u32[]{:S(2)}, u32[]{:S(2)}) collective-permute-start(bf16[16,1,512]{2,1,0:T(2,128)(2,1)S(1)} %get-tuple-element.8), channel_id=1, source_target_pairs={{0,1},{1,2},{2,3},{3,4},{4,5},{5,6},{6,7},{7,0},{8,9},{9,10},{10,1... | collective-permute-start | bytes 49160 | tf_op jit(solution)/shard_map/ppermute | solution.py:14
  14.5 3.1 %collective-permute-start.1 = (bf16[16,1,512]{2,1,0:T(2,128)(2,1)S(1)}, bf16[16,1,512]{2,1,0:T(2,128)(2,1)S(1)}, u32[]{:S(2)}, u32[]{:S(2)}) collective-permute-start(bf16[16,1,512]{2,1,0:T(2,128)(2,1)S(1)} %get-tuple-element.9), channel_id=1, source_target_pairs={{1,0},{2,1},{3,2},{4,3},{5,4},{6,5},{7,6},{0,7},{9,8},{10,9},{11,1... | collective-permute-start | bytes 49160 | tf_op jit(solution)/shard_map/ppermute | solution.py:15
  17.7 0.7 broadcast_multiply_fusion.2
  18.3 0.8 maximum_clamp_fusion
  19.1 2.6 %fusion.11 = f32[512,512]{1,0:T(8,128)} fusion(bf16[512,512]{1,0:T(8,128)(2,1)} %bitcast.16, bf16[1024,512]{1,0:T(8,128)(2,1)} %param.19), kind=kOutput, calls=%fused_computation.23 | convolution fusion | flops 268435456 | bytes 2097152 | tf_op jit(solution)/shard_map/dot_general | solution.py:103
  21.7 0.0 copy-done.3
  21.7 0.0 copy-start.8
  21.7 0.0 copy-start.1
  21.7 0.0 copy-start.7
  21.7 4.3 %fusion.9 = f32[2048,512]{1,0:T(8,128)} fusion(bf16[2048,512]{1,0:T(8,128)(2,1)S(1)} %copy-done.3, bf16[1536,512]{1,0:T(8,128)(2,1)} %param.16), kind=kOutput, calls=%fused_computation.21 | convolution fusion | flops 1073741824 | bytes 6815744 | tf_op jit(solution)/shard_map/dot_general | solution.py:84
  26.0 0.0 copy-done.8
  26.0 0.1 fusion.33
  26.1 0.0 collective-permute-done
  26.1 0.0 collective-permute-done.1
  26.1 0.0 copy-done.1
  26.2 1.5 %collective-permute-start.2 = (bf16[1,34,512]{2,1,0:T(8,128)(2,1)S(1)}, bf16[1,34,512]{2,1,0:T(8,128)(2,1)S(1)}, u32[]{:S(2)}, u32[]{:S(2)}) collective-permute-start(bf16[1,34,512]{2,1,0:T(8,128)(2,1)S(1)} %get-tuple-element.6), channel_id=1, source_target_pairs={{0,8},{8,16},{16,24},{1,9},{9,17},{17,25},{2,10},{10,18},{18,26},{... | collective-permute-start | bytes 104456 | tf_op jit(solution)/shard_map/ppermute | solution.py:14
  27.6 1.3 %collective-permute-start.3 = (bf16[1,34,512]{2,1,0:T(8,128)(2,1)S(1)}, bf16[1,34,512]{2,1,0:T(8,128)(2,1)S(1)}, u32[]{:S(2)}, u32[]{:S(2)}) collective-permute-start(bf16[1,34,512]{2,1,0:T(8,128)(2,1)S(1)} %get-tuple-element.7), channel_id=1, source_target_pairs={{8,0},{16,8},{24,16},{9,1},{17,9},{25,17},{10,2},{18,10},{26,18},{... | collective-permute-start | bytes 104456 | tf_op jit(solution)/shard_map/ppermute | solution.py:15
  28.9 0.0 copy-done.7
  29.0 2.4 %copy.13 = bf16[2048,512]{0,1:T(8,128)(2,1)} copy(bf16[2048,512]{1,0:T(8,128)(2,1)S(1)} %copy-done.3) | data formatting | bytes 4194304 | tf_op args[1]
  31.4 9.2 %gather_fusion.1 = bf16[2048,512]{1,0:T(8,128)(2,1)} fusion(bf16[512,512]{1,0:T(8,128)(2,1)S(1)} %bitcast.17, s32[2048]{0:T(1024)S(1)} %get-tuple-element.4), kind=kCustom, calls=%fused_computation.1 | custom fusion | bytes 4202496 | tf_op jit(solution)/shard_map/gather | solution.py:86
  40.6 0.0 collective-permute-done.2
  40.6 0.0 collective-permute-done.3
  40.6 0.3 pad_maximum_fusion.1
  40.9 1.0 reshape.49
  41.9 26.2 %all-gather.2.cloned.1.call-done = bf16[1024,512]{1,0:T(8,128)(2,1)} async-done(((bf16[32,512]{1,0:T(8,128)(2,1)}), bf16[1024,512]{1,0:T(8,128)(2,1)}) %all-gather.2.cloned.1.call-update) | async-done | bytes 1048592 | tf_op jit(solution)/shard_map/all_gather | solution.py:28
  68.1 1.7 %pad_maximum_fusion = bf16[1636,512]{1,0:T(8,128)(2,1)S(1)} fusion(bf16[1024,512]{1,0:T(8,128)(2,1)} %all-gather.2.cloned.1.call-done, bf16[612,512]{1,0:T(8,128)(2,1)} %reshape.49), kind=kLoop, calls=%fused_computation.9 | loop fusion | flops 3350528 | bytes 3350528 | tf_op jit(solution)/shard_map/concatenate | solution.py:60
  69.8 9.2 %gather_fusion = bf16[2048,512]{1,0:T(8,128)(2,1)} fusion(bf16[1636,512]{1,0:T(8,128)(2,1)S(1)} %pad_maximum_fusion, s32[2048]{0:T(1024)S(1)} %fusion.33), kind=kCustom, calls=%fused_computation | custom fusion | bytes 4202496 | tf_op jit(solution)/shard_map/gather | solution.py:85
  79.0 4.9 %fusion.7 = f32[2048,512]{1,0:T(8,128)} fusion(bf16[2048,512]{1,0:T(8,128)(2,1)} %gather_fusion, bf16[1536,512]{1,0:T(8,128)(2,1)} %param.16), kind=kOutput, calls=%fused_computation.19 | convolution fusion | flops 1073741824 | bytes 6815744 | tf_op jit(solution)/shard_map/dot_general | solution.py:89
  83.9 0.0 copy-done
  83.9 0.0 copy-start.4
  83.9 9.2 %fusion.37 = (f32[2048]{0:T(1024)S(1)}, f32[2048,512]{0,1:T(8,128)}) fusion(bf16[512,512]{1,0:T(8,128)(2,1)S(1)} %copy-done, f32[2048,512]{1,0:T(8,128)} %fusion.9, f32[2048,512]{1,0:T(8,128)} %fusion.7, bf16[2048,512]{1,0:T(8,128)(2,1)} %gather_fusion.1, bf16[1536,512]{1,0:T(8,128)(2,1)} %param.16), kind=kOutput, calls=%fused_computation.89 | convolution fusion | flops 2155870208 | bytes 15736832 | tf_op jit(solution)/shard_map/dot_general | solution.py:93
  93.1 0.0 copy-start.2
  93.1 0.0 copy-start.10
  93.1 2.8 %multiply_reduce_fusion = f32[2048]{0:T(1024)S(1)} fusion(f32[2048,512]{0,1:T(8,128)} %get-tuple-element.11, f32[2048]{0:T(1024)S(1)} %broadcast_multiply_fusion), kind=kLoop, calls=%fused_computation.4 | loop fusion | flops 3143680 | bytes 4210688 | tf_op jit(solution)/shard_map/reduce_sum | solution.py:23
  95.9 0.0 copy-done.4
  95.9 0.6 copy-done.2
  96.5 0.0 copy-done.10
  96.5 2.6 %select_convert_fusion = bf16[2048,512]{0,1:T(8,128)(2,1)} fusion(bf16[2048,512]{0,1:T(8,128)(2,1)S(1)} %copy-done.4, pred[2048]{0:T(1024)(128)(4,1)S(1)} %broadcast_compare_fusion, f32[512]{0:T(512)S(1)} %copy-done.10, f32[2048]{0:T(1024)S(1)} %add_rsqrt_fusion, f32[2048,512]{0,1:T(8,128)S(1)} %copy-done.2, f32[2048]{0:T(1024)S(1)} %broadcast_multiply_fusion), kind=kLoop, calls=%fused_computation.2 | loop fusion | flops 9437184 | bytes 8409088 | tf_op jit(solution)/shard_map/convert_element_type | solution.py:97
  99.1 0.0 copy-start.5
  99.1 4.0 %copy.14 = bf16[2048,512]{1,0:T(8,128)(2,1)} copy(bf16[2048,512]{0,1:T(8,128)(2,1)} %select_convert_fusion) | data formatting | bytes 4194304
  103.1 0.0 copy-done.5
  103.1 0.0 copy-start.6
  103.1 4.2 %multiply_convert_fusion.2 = bf16[512,512]{1,0:T(8,128)(2,1)S(1)} fusion(f32[512,512]{1,0:T(8,128)S(1)} %copy-done.5, s32[2048]{0:T(1024)S(1)} %get-tuple-element.5, bf16[1024,512]{1,0:T(8,128)(2,1)} %param.19, f32[2048,512]{0,1:T(8,128)} %get-tuple-element.11, f32[512]{0:T(512)S(1)} %copy-done.10, f32[2048]{0:T(1024)S(1)} %add_rsqrt_fusion, ...), kind=kOutput, calls=%fused_computation.15 | convolution fusion | flops 1349255168 | bytes 6318080 | tf_op jit(solution)/shard_map/dot_general | solution.py:105
  107.3 0.0 copy-done.6
  107.3 0.0 copy-start.9
  107.3 0.5 fusion.40
  107.9 0.3 multiply_reduce_fusion.1
  108.1 0.0 copy-done.9
  108.2 1.1 add_convert_fusion
  (6 shorter events, 0.1 us)
Async XLA Ops:
  7.2 76.7 %copy-start = (bf16[512,512]{1,0:T(8,128)(2,1)S(1)}, bf16[512,512]{1,0:T(8,128)(2,1)}, u32[]{:S(2)}) copy-start(bf16[512,512]{1,0:T(8,128)(2,1)} %param.17) | copy-start | bytes 1572868
  7.2 14.5 %copy-start.3 = (bf16[2048,512]{1,0:T(8,128)(2,1)S(1)}, bf16[2048,512]{1,0:T(8,128)(2,1)}, u32[]{:S(2)}) copy-start(bf16[2048,512]{1,0:T(8,128)(2,1)} %param.12) | copy-start | bytes 6291460
  7.2 61.0 %all-gather.2.cloned.1.call-start = ((), (), s32[]{:S(2)}) async-start(), calls=%async_computation | async-start | bytes 1081344 | tf_op jit(solution)/shard_map/all_gather | solution.py:28
  11.5 14.6 %collective-permute-start = (bf16[16,1,512]{2,1,0:T(2,128)(2,1)S(1)}, bf16[16,1,512]{2,1,0:T(2,128)(2,1)S(1)}, u32[]{:S(2)}, u32[]{:S(2)}) collective-permute-start(bf16[16,1,512]{2,1,0:T(2,128)(2,1)S(1)} %get-tuple-element.8), channel_id=1, source_target_pairs={{0,1},{1,2},{2,3},{3,4},{4,5},{5,6},{6,7},{7,0},{8,9},{9,10},{10,1... | collective-permute-start | bytes 49160 | tf_op jit(solution)/shard_map/ppermute | solution.py:14
  14.5 11.6 %collective-permute-start.1 = (bf16[16,1,512]{2,1,0:T(2,128)(2,1)S(1)}, bf16[16,1,512]{2,1,0:T(2,128)(2,1)S(1)}, u32[]{:S(2)}, u32[]{:S(2)}) collective-permute-start(bf16[16,1,512]{2,1,0:T(2,128)(2,1)S(1)} %get-tuple-element.9), channel_id=1, source_target_pairs={{1,0},{2,1},{3,2},{4,3},{5,4},{6,5},{7,6},{0,7},{9,8},{10,9},{11,1... | collective-permute-start | bytes 49160 | tf_op jit(solution)/shard_map/ppermute | solution.py:15
  21.7 4.3 %copy-start.8 = (s32[2048]{0:T(1024)S(1)}, s32[2048]{0:T(1024)}, u32[]{:S(2)}) copy-start(s32[2048]{0:T(1024)} %param.13) | copy-start | bytes 24580
  21.7 4.4 %copy-start.1 = (bf16[16,32,512]{2,1,0:T(8,128)(2,1)S(1)}, bf16[16,32,512]{2,1,0:T(8,128)(2,1)}, u32[]{:S(2)}) copy-start(bf16[16,32,512]{2,1,0:T(8,128)(2,1)} %param.11) | copy-start | bytes 1572868
  21.7 7.2 %copy-start.7 = (s32[2048]{0:T(1024)S(1)}, s32[2048]{0:T(1024)}, u32[]{:S(2)}) copy-start(s32[2048]{0:T(1024)} %param.14) | copy-start | bytes 24580
  26.2 14.4 %collective-permute-start.2 = (bf16[1,34,512]{2,1,0:T(8,128)(2,1)S(1)}, bf16[1,34,512]{2,1,0:T(8,128)(2,1)S(1)}, u32[]{:S(2)}, u32[]{:S(2)}) collective-permute-start(bf16[1,34,512]{2,1,0:T(8,128)(2,1)S(1)} %get-tuple-element.6), channel_id=1, source_target_pairs={{0,8},{8,16},{16,24},{1,9},{9,17},{17,25},{2,10},{10,18},{18,26},{... | collective-permute-start | bytes 104456 | tf_op jit(solution)/shard_map/ppermute | solution.py:14
  27.6 12.9 %collective-permute-start.3 = (bf16[1,34,512]{2,1,0:T(8,128)(2,1)S(1)}, bf16[1,34,512]{2,1,0:T(8,128)(2,1)S(1)}, u32[]{:S(2)}, u32[]{:S(2)}) collective-permute-start(bf16[1,34,512]{2,1,0:T(8,128)(2,1)S(1)} %get-tuple-element.7), channel_id=1, source_target_pairs={{8,0},{16,8},{24,16},{9,1},{17,9},{25,17},{10,2},{18,10},{26,18},{... | collective-permute-start | bytes 104456 | tf_op jit(solution)/shard_map/ppermute | solution.py:15
  83.9 12.0 %copy-start.4 = (bf16[2048,512]{0,1:T(8,128)(2,1)S(1)}, bf16[2048,512]{0,1:T(8,128)(2,1)}, u32[]{:S(2)}) copy-start(bf16[2048,512]{0,1:T(8,128)(2,1)} %copy.13) | copy-start | bytes 6291460
  93.1 3.4 %copy-start.2 = (f32[2048,512]{0,1:T(8,128)S(1)}, f32[2048,512]{0,1:T(8,128)}, u32[]{:S(2)}) copy-start(f32[2048,512]{0,1:T(8,128)} %get-tuple-element.11) | copy-start | bytes 12582916
  93.1 3.4 %copy-start.10 = (f32[512]{0:T(512)S(1)}, f32[512]{0:T(512)}, u32[]{:S(2)}) copy-start(f32[512]{0:T(512)} %param.18) | copy-start | bytes 6148
  99.1 4.0 %copy-start.5 = (f32[512,512]{1,0:T(8,128)S(1)}, f32[512,512]{1,0:T(8,128)}, u32[]{:S(2)}) copy-start(f32[512,512]{1,0:T(8,128)} %fusion.11) | copy-start | bytes 3145732
  103.1 4.2 %copy-start.6 = (bf16[512,512]{1,0:T(8,128)(2,1)S(1)}, bf16[512,512]{1,0:T(8,128)(2,1)}, u32[]{:S(2)}) copy-start(bf16[512,512]{1,0:T(8,128)(2,1)} %param.20) | copy-start | bytes 1572868
  107.3 0.8 copy-start.9
Sparse Core Ops, SparseCore 0:
  11.6 56.4 all-gather.1
where the time goes:
time: 117 us; the launch traced here: 116 us
  local copies, waits for them, and re-layouts  30.7 us (26%)
  waiting for transfers between devices  26.3 us (22%)
  matrix products  25.7 us (22%)
  between operations  14.2 us (12%)
  other arithmetic  10.2 us (9%)
  starting transfers between devices  8.94 us (8%)
    all_gather x1, waiting for transfers between devices, coarse_table(): return lax.all_gather(coarse_own, ('lat', 'lon'), axis=0, tiled=True)  26.2 us
    gather x1, local copies, waits for them, and re-layouts, per_device(): send_rows = lookup[table_index]  9.21 us
    dot_general x1, matrix products, per_device(): second_sum = jnp.dot(hidden, w_second, preferred_element_type=jnp.float32)  9.19 us
    gather x1, local copies, waits for them, and re-layouts, per_device(): recv_rows = own_rows[recv_index]  9.18 us
    unnamed x24, local copies, waits for them, and re-layouts  7.12 us
    dot_general x1, matrix products, per_device(): jnp.dot(send_rows, w_send, preferred_element_type=jnp.float32)  4.88 us
    ppermute x2, starting transfers between devices, padded(): before = lax.ppermute(last, axis, up)  4.5 us
    ppermute x2, starting transfers between devices, padded(): after = lax.ppermute(leading, axis, down)  4.4 us
  transfers between devices with their start and end apart: 5, of which 1 were waited for; matrix products, arithmetic and copies ran while one was open for 19% of the time, Pallas kernels for 0%

commit v1 on v0

v1 whole, which is shorter than its diff:
```python
import functools

import jax
import jax.numpy as jnp
from jax import lax
from jax.experimental import pallas as pl
from jax.experimental.pallas import tpu as pltpu
from jax.sharding import PartitionSpec as P

F32 = jnp.float32
BF16 = jnp.bfloat16
LANES = 128


def dot(a, b):
    return jnp.dot(a, b, preferred_element_type=F32)


def silu(value):
    half = 0.5 * value
    return half * (1.0 + jnp.tanh(half))


def layer_norm(values, gain_vec):
    average = jnp.mean(values, -1, keepdims=True)
    centred = values - average
    spread = jnp.mean(centred * centred, -1, keepdims=True)
    return centred * lax.rsqrt(spread + 1e-05) * gain_vec


def compute_kernel(
    group,
    block_len,
    tile_nodes,
    tile_ref,
    edge_ref,
    send_ref,
    recv_ref,
    table_ref,
    own_ref,
    w_first_ref,
    w_second_ref,
    edge_gain_ref,
    w_node_first_ref,
    w_node_second_ref,
    node_gain_ref,
    node_out_ref,
    edge_out_ref,
    total_ref,
):
    step = pl.program_id(0)
    features = edge_ref.shape[1]
    table_len = table_ref.shape[0]

    @pl.when(step == 0)
    def _():
        total_ref[...] = jnp.zeros_like(total_ref)

    def columns_of(row, width):
        spread = jnp.broadcast_to(row, (LANES, block_len)).T
        lane = lax.broadcasted_iota(jnp.int32, (block_len, LANES), 1)
        parts = [
            jnp.where(spread == lane + j * LANES, 1.0, 0.0).astype(BF16)
            for j in range(width // LANES)
        ]
        return spread, jnp.concatenate(parts, axis=1)

    sent, received, live = [], [], []
    for i in range(group):
        _, hot = columns_of(send_ref[i], table_len)
        sent.append(hot)
        tile = tile_ref[step * group + i]
        start = pl.multiple_of(tile * tile_nodes, tile_nodes)
        spread, hot_recv = columns_of(recv_ref[i], tile_nodes)
        live.append(jnp.concatenate([spread] * (features // LANES), axis=1))
        received.append(dot(hot_recv, own_ref[pl.ds(start, tile_nodes), :]).astype(BF16))
    edges = edge_ref[...]
    send_rows = dot(jnp.concatenate(sent, axis=0), table_ref[...]).astype(BF16)
    recv_rows = jnp.concatenate(received, axis=0)
    first = (
        dot(edges, w_first_ref[:features, :])
        + dot(recv_rows, w_first_ref[2 * features :, :])
        + dot(send_rows, w_first_ref[features : 2 * features, :])
    )
    hidden = silu(first).astype(BF16)
    message = layer_norm(dot(hidden, w_second_ref[...]), edge_gain_ref[...]).astype(BF16)
    updated = edges.astype(F32) + message.astype(F32)
    edge_out_ref[...] = jnp.where(jnp.concatenate(live, axis=0) >= 0, updated, 0.0).astype(BF16)
    for i in range(group):
        tile = tile_ref[step * group + i]
        start = pl.multiple_of(tile * tile_nodes, tile_nodes)
        node = lax.broadcasted_iota(jnp.int32, (tile_nodes, block_len), 0)
        hot = jnp.where(node == recv_ref[i], 1.0, 0.0).astype(BF16)
        total_ref[pl.ds(start, tile_nodes), :] += dot(
            hot, message[i * block_len : (i + 1) * block_len, :]
        )

    @pl.when(step == pl.num_programs(0) - 1)
    def _():
        own = own_ref[...]
        node_first = dot(own, w_node_first_ref[:features, :]) + dot(
            total_ref[...].astype(BF16), w_node_first_ref[features:, :]
        )
        node_hidden = silu(node_first).astype(BF16)
        node_second = dot(node_hidden, w_node_second_ref[...])
        node_out_ref[...] = (
            own.astype(F32) + layer_norm(node_second, node_gain_ref[...])
        ).astype(BF16)


def compute(
    block_tile, edges, senders, receivers, table, own, weights, tile_nodes
):
    blocks = block_tile.shape[0]
    edge_count, features = edges.shape
    block_len = edge_count // blocks
    node_count = own.shape[0]
    group = 4 if blocks % 4 == 0 else 1
    whole = pl.BlockSpec(memory_space=pltpu.VMEM)
    index = pl.BlockSpec((group, 1, block_len), lambda i, tiles: (i, 0, 0))
    rows = pl.BlockSpec((group * block_len, features), lambda i, tiles: (i, 0))
    return pl.pallas_call(
        functools.partial(compute_kernel, group, block_len, tile_nodes),
        grid_spec=pltpu.PrefetchScalarGridSpec(
            num_scalar_prefetch=1,
            grid=(blocks // group,),
            in_specs=[rows, index, index] + [whole] * 8,
            out_specs=[pl.BlockSpec((node_count, features), lambda i, tiles: (0, 0)), rows],
            scratch_shapes=[pltpu.VMEM((node_count, features), F32)],
        ),
        out_shape=[
            jax.ShapeDtypeStruct((node_count, features), BF16),
            jax.ShapeDtypeStruct((edge_count, features), BF16),
        ],
        compiler_params=pltpu.CompilerParams(
            dimension_semantics=("arbitrary",), vmem_limit_bytes=56 * 1024 * 1024
        ),
    )(
        block_tile,
        edges,
        senders.reshape(blocks, 1, block_len),
        receivers.reshape(blocks, 1, block_len),
        table,
        own,
        *weights,
    )


def shifted(value, axis, step, wrap):
    devices = lax.axis_size(axis)
    pairs = [(i, (i + step) % devices) for i in range(devices) if wrap or 0 <= i + step < devices]
    return lax.ppermute(value, axis, pairs)


def border_rows(own, patch_rows, patch_cols):
    count = patch_rows * patch_cols
    coarse_rows, coarse_cols = patch_rows // 4, patch_cols // 4
    coarse = coarse_rows * coarse_cols
    pick = lax.broadcasted_iota(jnp.int32, (coarse + 2 * patch_rows, count), 0)
    node = lax.broadcasted_iota(jnp.int32, (coarse + 2 * patch_rows, count), 1)
    from_coarse = pick // coarse_cols * 4 * patch_cols + pick % coarse_cols * 4
    side = pick - coarse
    from_side = jnp.where(
        side < patch_rows, side * patch_cols, (side - patch_rows) * patch_cols + patch_cols - 1
    )
    hot = (node == jnp.where(pick < coarse, from_coarse, from_side)).astype(BF16)
    return dot(hot, own).astype(BF16)


def per_device(
    node_latent,
    edge_latent,
    sender,
    receiver,
    block_tile,
    w_first,
    w_second,
    edge_gain,
    w_node_first,
    w_node_second,
    node_gain,
):
    patch_rows, patch_cols, features = node_latent.shape
    lat_count, lon_count = lax.axis_size("lat"), lax.axis_size("lon")
    lat_index, lon_index = lax.axis_index("lat"), lax.axis_index("lon")
    grid_cols = patch_cols * lon_count
    node_count = patch_rows * patch_cols
    coarse_per = patch_rows // 4 * (patch_cols // 4)
    own = node_latent.reshape(node_count, features)
    picked = border_rows(own, patch_rows, patch_cols)
    near, table_len = table_layout(patch_rows, patch_cols, coarse_per * lat_count * lon_count)
    table = build_table(own, picked, patch_rows, patch_cols, near, table_len)

    send_row, send_col = sender // grid_cols, sender % grid_cols
    row = send_row - lat_index * patch_rows
    col = (send_col - lon_index * patch_cols + 1) % grid_cols - 1
    is_near = (row >= -1) & (row <= patch_rows) & (col <= patch_cols)
    inside = (col >= 0) & (col < patch_cols)
    left, right, top, bottom, corners, coarse_at = near
    side = jnp.where(col < 0, left, right)
    corner_side = jnp.where(col < 0, 0, 16)
    top_index = jnp.where(inside, top + col, corners + corner_side + 7)
    bottom_index = jnp.where(inside, bottom + col, corners + corner_side + 8)
    middle = jnp.where(inside, row * patch_cols + col, side + row)
    near_index = jnp.where(row < 0, top_index, jnp.where(row >= patch_rows, bottom_index, middle))
    far_index = (
        coarse_at
        + (send_row // patch_rows * lon_count + send_col // patch_cols) * coarse_per
        + send_row % patch_rows // 4 * (patch_cols // 4)
        + send_col % patch_cols // 4
    )
    senders = jnp.where(sender < 0, -1, jnp.where(is_near, near_index, far_index))
    weights = (
        w_first,
        w_second,
        edge_gain.reshape(1, -1),
        w_node_first,
        w_node_second,
        node_gain.reshape(1, -1),
    )
    node_out, edge_out = compute(
        block_tile, edge_latent, senders, receiver, table, own, weights, 4 * patch_cols
    )
    return node_out.reshape(patch_rows, patch_cols, features), edge_out


def table_layout(patch_rows, patch_cols, coarse_count):
    left = patch_rows * patch_cols
    right = left + patch_rows
    top = right + patch_rows
    bottom = top + patch_cols
    corners = bottom + patch_cols
    coarse_at = corners + 32
    table_len = -(-(coarse_at + coarse_count) // LANES) * LANES
    return (left, right, top, bottom, corners, coarse_at), table_len


def build_table(own, picked, patch_rows, patch_cols, near, table_len):
    features = own.shape[1]
    coarse_per = picked.shape[0] - 2 * patch_rows
    coarse_own = picked[:coarse_per]
    first_col = picked[coarse_per : coarse_per + patch_rows]
    last_col = picked[coarse_per + patch_rows :]
    coarse = lax.all_gather(coarse_own, ("lat", "lon"), axis=0, tiled=True)
    left = shifted(last_col, "lon", 1, True)
    right = shifted(first_col, "lon", -1, True)
    from_north = shifted(
        jnp.concatenate([own[-patch_cols:], left[-8:], right[-8:]]), "lat", 1, False
    )
    from_south = shifted(jnp.concatenate([own[:patch_cols], left[:8], right[:8]]), "lat", -1, False)
    n, nw, ne = from_north[:patch_cols], from_north[patch_cols:-8], from_north[-8:]
    s, sw, se = from_south[:patch_cols], from_south[patch_cols:-8], from_south[-8:]
    pad = jnp.zeros((table_len - near[5] - coarse.shape[0], features), BF16)
    return jnp.concatenate([own, left, right, n, s, nw, sw, ne, se, coarse, pad], axis=0)


def solution(mesh):
    return jax.shard_map(
        per_device,
        mesh=mesh,
        in_specs=(
            P("lat", "lon", None),
            P(("lat", "lon"), None),
            P(("lat", "lon")),
            P(("lat", "lon")),
            P(("lat", "lon")),
            P(),
            P(),
            P(),
            P(),
            P(),
            P(),
        ),
        out_specs=(P("lat", "lon", None), P(("lat", "lon"), None)),
        check_vma=False,
    )
```

time: 117 us -> 95.9 us (0.82)
  local copies, waits for them, and re-layouts: 30.7 us -> 5 us
  matrix products: 25.7 us -> 1.33 us
  waiting for transfers between devices: 26.3 us -> 46.6 us
  Pallas kernels: 0 us -> 18.1 us
  other arithmetic: 10.2 us -> 1.38 us
    dot_general x6 -> x1, matrix products: 25.7 us -> 1.33 us  [dot(): return jnp.dot(a, b, preferred_element_type=F32)]
    gather x2 -> x0, local copies, waits for them, and re-layouts: 18.4 us -> none  [the longest x1 9.21 us: per_device(): send_rows = lookup[table_index]]
    pallas_call x0 -> x1, Pallas kernels: none -> 18.1 us  [compute(): pl.pallas_call(functools.partial(compute_kernel, group, block_len, tile_n...]
    all_gather x1, waiting for transfers between devices: 26.2 us -> 43.1 us  [build_table(): coarse = lax.all_gather(coarse_own, ('lat', 'lon'), axis=0, tiled=True)]
    unnamed x24 -> x11, local copies, waits for them, and re-layouts: 7.12 us -> 2.3 us
    convert_element_type x2 -> x0, other arithmetic: 3.63 us -> none  [the longest x1 2.57 us: per_device(): updated = jnp.where(live_slot[:, None], edge_latent.astype(jnp.float32) +...]
    ppermute x4, waiting for transfers between devices: 0.01 us -> 3.44 us  [shifted(): return lax.ppermute(value, axis, pairs)]
    reduce_sum x2 -> x0, other arithmetic: 3.05 us -> none  [layer_norm(): spread = jnp.mean(centred * centred, -1, keepdims=True)]
  transfers between devices with their start and end apart: 5 -> 5, of which waited for: 1 -> 2; matrix products, arithmetic and copies ran while one was open for 19% -> 4% of each run, Pallas kernels for 0% -> 0%
where the time goes in v1:
time: 95.9 us; the launch traced here: 95.5 us
  waiting for transfers between devices  46.6 us (49%)
  Pallas kernels  18.1 us (19%)
  between operations  14.2 us (15%)
  starting transfers between devices  8.94 us (9%)
  local copies, waits for them, and re-layouts  5 us (5%)
  other arithmetic  1.38 us (1%)
  matrix products  1.33 us (1%)
    all_gather x1, waiting for transfers between devices, build_table(): coarse = lax.all_gather(coarse_own, ('lat', 'lon'), axis=0, tiled=True)  43.1 us
    pallas_call x1, Pallas kernels, compute(): pl.pallas_call(functools.partial(compute_kernel, group, block_len, tile_n...  18.1 us
    ppermute x4, starting transfers between devices, shifted(): return lax.ppermute(value, axis, pairs)  8.9 us
    ppermute x4, waiting for transfers between devices, shifted(): return lax.ppermute(value, axis, pairs)  3.44 us
    unnamed x11, local copies, waits for them, and re-layouts  2.3 us
  transfers between devices with their start and end apart: 5, of which 2 were waited for; matrix products, arithmetic and copies ran while one was open for 4% of the time, Pallas kernels for 0%

profile of v1, /device:TPU:0, one launch (start us, length us, event | category | flops | bytes accessed | tf_op | source)
XLA Modules:
  0.0 95.5 jit_solution(11633666131603514823)
XLA Ops:
  7.2 0.0 all-gather.2.cloned.1.call-start
  7.3 1.3 %convolution_convert_fusion = bf16[64,512]{1,0:T(8,128)(2,1)S(1)} fusion(bf16[512,512]{1,0:T(8,128)(2,1)} %bitcast.11, s32[64]{0:T(128)S(1)} %get-tuple-element.21, s32[64]{0:T(128)S(1)} %get-tuple-element.20, s32[64]{0:T(128)S(1)} %get-tuple-element.17, s32[64]{0:T(128)S(1)} %get-tuple-element.22, s32[64]{0:T(128)S(1)} %get-tuple-element.16, ...), kind=kOutput, calls=%fused_computation | convolution fusion | flops 33849344 | bytes 591616 | tf_op jit(solution)/shard_map/dot_general | solution.py:16
  8.6 3.0 %collective-permute-start = (bf16[16,512]{1,0:T(8,128)(2,1)S(1)}, bf16[16,512]{1,0:T(8,128)(2,1)S(1)}, u32[]{:S(2)}, u32[]{:S(2)}) collective-permute-start(bf16[16,512]{1,0:T(8,128)(2,1)S(1)} %get-tuple-element.9), channel_id=1, source_target_pairs={{0,1},{1,2},{2,3},{3,4},{4,5},{5,6},{6,7},{7,0},{8,9},{9,10},{10,1... | collective-permute-start | bytes 49160 | tf_op jit(solution)/shard_map/ppermute | solution.py:152
  11.7 3.1 %collective-permute-start.1 = (bf16[16,512]{1,0:T(8,128)(2,1)S(1)}, bf16[16,512]{1,0:T(8,128)(2,1)S(1)}, u32[]{:S(2)}, u32[]{:S(2)}) collective-permute-start(bf16[16,512]{1,0:T(8,128)(2,1)S(1)} %get-tuple-element.8), channel_id=1, source_target_pairs={{0,7},{1,0},{2,1},{3,2},{4,3},{5,4},{6,5},{7,6},{8,15},{9,8},{10,9... | collective-permute-start | bytes 49160 | tf_op jit(solution)/shard_map/ppermute | solution.py:152
  14.8 0.6 slice.80
  15.4 0.0 all-gather.2.cloned.1.call-update
  15.4 0.8 slice_bitcast_fusion
  16.2 1.3 %fusion.15 = s32[2048]{0:T(1024)} fusion(s32[2048]{0:T(1024)} %param.13, s32[]{:T(128)S(6)} %mul.36, s32[]{:T(128)S(6)} %mul.35), kind=kLoop, calls=%fused_computation.59 | loop fusion | flops 278528 | bytes 16392 | tf_op jit(solution)/shard_map/jit(_where)/select_n | solution.py:212
  17.5 1.1 %constant_dynamic-update-slice_fusion.7 = bf16[1664,512]{1,0:T(8,128)(2,1)S(1)} fusion(bf16[512,512]{1,0:T(8,128)(2,1)} %bitcast.12), kind=kLoop, calls=%fused_computation.27 | loop fusion | bytes 1048576
  18.6 0.0 collective-permute-done
  18.6 0.0 collective-permute-done.1
  18.7 1.5 %collective-permute-start.2 = (bf16[48,512]{1,0:T(8,128)(2,1)S(1)}, bf16[48,512]{1,0:T(8,128)(2,1)S(1)}, u32[]{:S(2)}, u32[]{:S(2)}) collective-permute-start(bf16[48,512]{1,0:T(8,128)(2,1)S(1)} %pad_maximum_fusion), channel_id=1, source_target_pairs={{0,8},{8,16},{16,24},{1,9},{9,17},{17,25},{2,10},{10,18},{18,26},{... | collective-permute-start | bytes 147464 | tf_op jit(solution)/shard_map/ppermute | solution.py:152
  20.2 1.3 %collective-permute-start.3 = (bf16[48,512]{1,0:T(8,128)(2,1)S(1)}, bf16[48,512]{1,0:T(8,128)(2,1)S(1)}, u32[]{:S(2)}, u32[]{:S(2)}) collective-permute-start(bf16[48,512]{1,0:T(8,128)(2,1)S(1)} %pad_maximum_fusion.1), channel_id=1, source_target_pairs={{8,0},{16,8},{24,16},{9,1},{17,9},{25,17},{10,2},{18,10},{26,18},{... | collective-permute-start | bytes 147464 | tf_op jit(solution)/shard_map/ppermute | solution.py:152
  21.5 0.0 collective-permute-done.2
  21.5 3.4 %collective-permute-done.3 = bf16[48,512]{1,0:T(8,128)(2,1)S(1)} collective-permute-done((bf16[48,512]{1,0:T(8,128)(2,1)S(1)}, bf16[48,512]{1,0:T(8,128)(2,1)S(1)}, u32[]{:S(2)}, u32[]{:S(2)}) %collective-permute-start.3) | collective-permute-done | bytes 49184 | tf_op jit(solution)/shard_map/ppermute | solution.py:152
  25.0 43.1 %all-gather.2.cloned.1.call-done = bf16[1024,512]{1,0:T(8,128)(2,1)} async-done(((bf16[32,512]{1,0:T(8,128)(2,1)}), bf16[1024,512]{1,0:T(8,128)(2,1)}) %all-gather.2.cloned.1.call-update) | async-done | bytes 1048592 | tf_op jit(solution)/shard_map/all_gather | solution.py:244
  68.1 1.3 %constant_dynamic-update-slice_fusion.table_ref = bf16[1664,512]{1,0:T(8,128)(2,1)S(1)} fusion(bf16[1664,512]{1,0:T(8,128)(2,1)S(1)} %constant_dynamic-update-slice_fusion.1, bf16[1024,512]{1,0:T(8,128)(2,1)} %all-gather.2.cloned.1.call-done), kind=kLoop, calls=%fused_computation.20 | loop fusion | bytes 2097152 | tf_op jit(solution)/shard_map/concatenate | solution.py:254
  69.4 0.0 copy-start
  69.4 1.2 %copy-done = bf16[1664,512]{1,0:T(8,128)(2,1)} copy-done((bf16[1664,512]{1,0:T(8,128)(2,1)}, bf16[1664,512]{1,0:T(8,128)(2,1)S(1)}, u32[]{:S(2)}) %copy-start) | copy-done | bytes 1703960
  70.6 18.1 %shard_map.122 = (bf16[512,512]{1,0:T(8,128)(2,1)}, bf16[2048,512]{1,0:T(8,128)(2,1)}) custom-call(s32[16]{0:T(128)} %tile_ref.1, bf16[2048,512]{1,0:T(8,128)(2,1)} %edge_ref.1, s32[16,1,128]{2,1,0:T(1,128)} %bitcast.14, s32[16,1,128]{2,1,0:T(1,128)} %bitcast.15, bf16[1664,512]{1,0:T(8,128)(2,1)} %copy-done, bf16[512,512]{1,0:T(8,128)(2,1)} %bitcast.13, ...), custom_call_target="tpu_custom_call" | custom-call | tf_op jit(solution)/shard_map/pallas_call | solution.py:122
  (18 shorter events, 0.1 us)
Async XLA Ops:
  7.2 61.0 %all-gather.2.cloned.1.call-start = ((), (), s32[]{:S(2)}) async-start(), calls=%async_computation | async-start | bytes 1081344 | tf_op jit(solution)/shard_map/all_gather | solution.py:244
  8.6 10.0 %collective-permute-start = (bf16[16,512]{1,0:T(8,128)(2,1)S(1)}, bf16[16,512]{1,0:T(8,128)(2,1)S(1)}, u32[]{:S(2)}, u32[]{:S(2)}) collective-permute-start(bf16[16,512]{1,0:T(8,128)(2,1)S(1)} %get-tuple-element.9), channel_id=1, source_target_pairs={{0,1},{1,2},{2,3},{3,4},{4,5},{5,6},{6,7},{7,0},{8,9},{9,10},{10,1... | collective-permute-start | bytes 49160 | tf_op jit(solution)/shard_map/ppermute | solution.py:152
  11.7 7.0 %collective-permute-start.1 = (bf16[16,512]{1,0:T(8,128)(2,1)S(1)}, bf16[16,512]{1,0:T(8,128)(2,1)S(1)}, u32[]{:S(2)}, u32[]{:S(2)}) collective-permute-start(bf16[16,512]{1,0:T(8,128)(2,1)S(1)} %get-tuple-element.8), channel_id=1, source_target_pairs={{0,7},{1,0},{2,1},{3,2},{4,3},{5,4},{6,5},{7,6},{8,15},{9,8},{10,9... | collective-permute-start | bytes 49160 | tf_op jit(solution)/shard_map/ppermute | solution.py:152
  18.7 2.8 %collective-permute-start.2 = (bf16[48,512]{1,0:T(8,128)(2,1)S(1)}, bf16[48,512]{1,0:T(8,128)(2,1)S(1)}, u32[]{:S(2)}, u32[]{:S(2)}) collective-permute-start(bf16[48,512]{1,0:T(8,128)(2,1)S(1)} %pad_maximum_fusion), channel_id=1, source_target_pairs={{0,8},{8,16},{16,24},{1,9},{9,17},{17,25},{2,10},{10,18},{18,26},{... | collective-permute-start | bytes 147464 | tf_op jit(solution)/shard_map/ppermute | solution.py:152
  20.2 4.8 %collective-permute-start.3 = (bf16[48,512]{1,0:T(8,128)(2,1)S(1)}, bf16[48,512]{1,0:T(8,128)(2,1)S(1)}, u32[]{:S(2)}, u32[]{:S(2)}) collective-permute-start(bf16[48,512]{1,0:T(8,128)(2,1)S(1)} %pad_maximum_fusion.1), channel_id=1, source_target_pairs={{8,0},{16,8},{24,16},{9,1},{17,9},{25,17},{10,2},{18,10},{26,18},{... | collective-permute-start | bytes 147464 | tf_op jit(solution)/shard_map/ppermute | solution.py:152
  69.4 1.2 %copy-start = (bf16[1664,512]{1,0:T(8,128)(2,1)}, bf16[1664,512]{1,0:T(8,128)(2,1)S(1)}, u32[]{:S(2)}) copy-start(bf16[1664,512]{1,0:T(8,128)(2,1)S(1)} %constant_dynamic-update-slice_fusion.table_ref) | copy-start | bytes 5111812
Sparse Core Ops, SparseCore 0:
  15.5 52.5 all-gather.1

commit v2 on v1

--- a/solution.py
+++ b/solution.py
@@ -50,7 +50,8 @@
 ):
     step = pl.program_id(0)
     features = edge_ref.shape[1]
-    table_len = table_ref.shape[0]
+    node_count = own_ref.shape[0]
+    table_len = node_count + table_ref.shape[0]
 
     @pl.when(step == 0)
     def _():
@@ -75,7 +76,10 @@
         live.append(jnp.concatenate([spread] * (features // LANES), axis=1))
         received.append(dot(hot_recv, own_ref[pl.ds(start, tile_nodes), :]).astype(BF16))
     edges = edge_ref[...]
-    send_rows = dot(jnp.concatenate(sent, axis=0), table_ref[...]).astype(BF16)
+    sent = jnp.concatenate(sent, axis=0)
+    send_rows = (
+        dot(sent[:, :node_count], own_ref[...]) + dot(sent[:, node_count:], table_ref[...])
+    ).astype(BF16)
     recv_rows = jnp.concatenate(received, axis=0)
     first = (
         dot(edges, w_first_ref[:features, :])
@@ -146,12 +150,6 @@
     )
 
 
-def shifted(value, axis, step, wrap):
-    devices = lax.axis_size(axis)
-    pairs = [(i, (i + step) % devices) for i in range(devices) if wrap or 0 <= i + step < devices]
-    return lax.ppermute(value, axis, pairs)
-
-
 def border_rows(own, patch_rows, patch_cols):
     count = patch_rows * patch_cols
     coarse_rows, coarse_cols = patch_rows // 4, patch_cols // 4
@@ -235,23 +233,146 @@
     return (left, right, top, bottom, corners, coarse_at), table_len
 
 
+def exchange_kernel(patch_rows, patch_cols, near, own_ref, picked_ref, table_ref, *sems):
+    halo_send, halo_recv, far_send, far_recv, pair_send, pair_recv, ready = sems
+    lat_count, lon_count = lax.axis_size("lat"), lax.axis_size("lon")
+    lat, lon = lax.axis_index("lat"), lax.axis_index("lon")
+    node_count = own_ref.shape[0]
+    left, right, top, bottom, corners, coarse_at = near
+    per = picked_ref.shape[0] - 2 * patch_rows
+    cores = 2 if lat_count % 2 == 0 else 1
+    chips = lat_count * lon_count // cores
+    core = lax.rem(lat, cores)
+    chip = lax.div(lat, cores) * lon_count + lon
+
+    def place(which, on_core):
+        return lax.div(which, lon_count) * cores + on_core, lax.rem(which, lon_count)
+
+    def slot(which, on_core):
+        at_lat, at_lon = place(which, on_core)
+        start = coarse_at + (at_lat * lon_count + at_lon) * per
+        return table_ref.at[pl.ds(pl.multiple_of(start, 8), per), :]
+
+    def copy(source, target, send_sem, recv_sem, at_lat, at_lon):
+        return pltpu.make_async_remote_copy(
+            src_ref=source,
+            dst_ref=target,
+            send_sem=send_sem,
+            recv_sem=recv_sem,
+            device_id={"lat": at_lat, "lon": at_lon},
+            device_id_type=pl.DeviceIdType.MESH,
+        )
+
+    coarse_own = picked_ref.at[pl.ds(0, per), :]
+
+    def far_out(k):
+        at_lat, at_lon = place(lax.rem(chip + k, chips), core)
+        return copy(coarse_own, slot(chip, core), far_send.at[k], far_recv.at[k], at_lat, at_lon)
+
+    def far_in(k):
+        origin = lax.rem(chip + chips - k, chips)
+        at_lat, at_lon = place(origin, core)
+        return copy(coarse_own, slot(origin, core), far_send.at[k], far_recv.at[k], at_lat, at_lon)
+
+    def pair(k, source_core):
+        origin = lax.rem(chip + chips - k, chips)
+        block = slot(origin, source_core)
+        return copy(block, block, pair_send.at[k], pair_recv.at[k], lat + 1 - 2 * core, lon)
+
+    first, last = per, per + patch_rows
+    halos = (
+        (picked_ref, last, patch_rows, left, 0, 1),
+        (picked_ref, first, patch_rows, right, 0, -1),
+        (own_ref, node_count - patch_cols, patch_cols, top, 1, 0),
+        (own_ref, 0, patch_cols, bottom, -1, 0),
+        (picked_ref, last + patch_rows - 8, 8, corners, 1, 1),
+        (picked_ref, last, 8, corners + 8, -1, 1),
+        (picked_ref, first + patch_rows - 8, 8, corners + 16, 1, -1),
+        (picked_ref, first, 8, corners + 24, -1, -1),
+    )
+
+    def halo(i):
+        ref, start, size, target, step_lat, step_lon = halos[i]
+        at_lat = lax.rem(lat + step_lat + lat_count, lat_count)
+        at_lon = lax.rem(lon + step_lon + lon_count, lon_count)
+        return copy(
+            ref.at[start : start + size, :],
+            table_ref.at[target : target + size, :],
+            halo_send.at[i],
+            halo_recv.at[i],
+            at_lat,
+            at_lon,
+        )
+
+    def sends(i):
+        there = lat + halos[i][4]
+        return (there >= 0) & (there < lat_count)
+
+    def receives(i):
+        origin = lat - halos[i][4]
+        return (origin >= 0) & (origin < lat_count)
+
+    lax.fori_loop(1, chips, lambda k, c: (far_out(k).start(), c)[1], 0)
+    if cores == 2:
+        own_pair = copy(
+            coarse_own, slot(chip, core), pair_send.at[0], pair_recv.at[0], lat + 1 - 2 * core, lon
+        )
+        own_pair.start()
+    for i in range(len(halos)):
+        pl.when(sends(i))(lambda i=i: halo(i).start())
+
+    local = pltpu.make_async_copy(coarse_own, slot(chip, core), ready)
+    local.start()
+    for i, (_, _, size, target, _, _) in enumerate(halos):
+
+        @pl.when(jnp.logical_not(receives(i)))
+        def _():
+            table_ref[target : target + size, :] = jnp.zeros((size, table_ref.shape[1]), BF16)
+
+    used = coarse_at + lat_count * lon_count * per
+    if used < table_ref.shape[0]:
+        table_ref[used:, :] = jnp.zeros((table_ref.shape[0] - used, table_ref.shape[1]), BF16)
+
+    def relay(k, c):
+        far_in(k).wait_recv()
+        if cores == 2:
+            pair(k, core).start()
+        return c
+
+    lax.fori_loop(1, chips, relay, 0)
+    local.wait()
+    for i in range(len(halos)):
+        pl.when(receives(i))(lambda i=i: halo(i).wait_recv())
+        pl.when(sends(i))(lambda i=i: halo(i).wait_send())
+
+    def finish(k, c):
+        far_out(k).wait_send()
+        if cores == 2:
+            pair(k, core).wait_send()
+            pair(k, 1 - core).wait_recv()
+        return c
+
+    lax.fori_loop(1, chips, finish, 0)
+    if cores == 2:
+        own_pair.wait_send()
+        pair(0, 1 - core).wait_recv()
+
+
 def build_table(own, picked, patch_rows, patch_cols, near, table_len):
-    features = own.shape[1]
-    coarse_per = picked.shape[0] - 2 * patch_rows
-    coarse_own = picked[:coarse_per]
-    first_col = picked[coarse_per : coarse_per + patch_rows]
-    last_col = picked[coarse_per + patch_rows :]
-    coarse = lax.all_gather(coarse_own, ("lat", "lon"), axis=0, tiled=True)
-    left = shifted(last_col, "lon", 1, True)
-    right = shifted(first_col, "lon", -1, True)
-    from_north = shifted(
-        jnp.concatenate([own[-patch_cols:], left[-8:], right[-8:]]), "lat", 1, False
-    )
-    from_south = shifted(jnp.concatenate([own[:patch_cols], left[:8], right[:8]]), "lat", -1, False)
-    n, nw, ne = from_north[:patch_cols], from_north[patch_cols:-8], from_north[-8:]
-    s, sw, se = from_south[:patch_cols], from_south[patch_cols:-8], from_south[-8:]
-    pad = jnp.zeros((table_len - near[5] - coarse.shape[0], features), BF16)
-    return jnp.concatenate([own, left, right, n, s, nw, sw, ne, se, coarse, pad], axis=0)
+    offset = own.shape[0]
+    near = tuple(at - offset for at in near)
+    chips = lax.axis_size("lat") * lax.axis_size("lon")
+    sems = [pltpu.SemaphoreType.DMA((8,))] * 2 + [pltpu.SemaphoreType.DMA((chips,))] * 4
+    return pl.pallas_call(
+        functools.partial(exchange_kernel, patch_rows, patch_cols, near),
+        in_specs=[pl.BlockSpec(memory_space=pltpu.VMEM)] * 2,
+        out_specs=pl.BlockSpec(memory_space=pltpu.VMEM),
+        out_shape=jax.ShapeDtypeStruct((table_len - offset, own.shape[1]), BF16),
+        scratch_shapes=sems + [pltpu.SemaphoreType.DMA],
+        compiler_params=pltpu.CompilerParams(
+            has_side_effects=True, vmem_limit_bytes=24 * 1024 * 1024
+        ),
+    )(own, picked)
 
 
 def solution(mesh):

time: 95.9 us -> 48 us (0.50)
  waiting for transfers between devices: 46.6 us -> 0 us
  Pallas kernels: 18.1 us -> 42.3 us
  between operations: 14.2 us -> 0.69 us
  starting transfers between devices: 8.94 us -> 0 us
  local copies, waits for them, and re-layouts: 5 us -> 2.05 us
    all_gather x1 -> x0, waiting for transfers between devices: 43.1 us -> none  [build_table(): coarse = lax.all_gather(coarse_own, ('lat', 'lon'), axis=0, tiled=True)]
    pallas_call x0 -> x1, Pallas kernels: none -> 24.4 us  [build_table(): pl.pallas_call(functools.partial(exchange_kernel, patch_rows, patch_cols,...]
    ppermute x4 -> x0, starting transfers between devices: 8.9 us -> none  [shifted(): return lax.ppermute(value, axis, pairs)]
    ppermute x4 -> x0, waiting for transfers between devices: 3.44 us -> none  [shifted(): return lax.ppermute(value, axis, pairs)]
    slice x5 -> x0, local copies, waits for them, and re-layouts: 1.41 us -> none  [the longest x1 0.78 us: build_table(): own[:patch_cols]]
    concatenate x1 -> x0, local copies, waits for them, and re-layouts: 1.29 us -> none  [build_table(): jnp.concatenate([own, left, right, n, s, nw, sw, ne, se, coarse, pad], ax...]
    unnamed x11 -> x4, local copies, waits for them, and re-layouts: 2.3 us -> 2.05 us
  transfers between devices with their start and end apart: 5 -> 0, of which waited for: 2 -> 0; matrix products, arithmetic and copies ran while one was open for 4% -> 0% of each run, Pallas kernels for 0% -> 0%
where the time goes in v2:
time: 48 us; the launch traced here: 47.8 us
  Pallas kernels  42.3 us (88%)
  local copies, waits for them, and re-layouts  2.05 us (4%)
  other arithmetic  1.38 us (3%)
  matrix products  1.33 us (3%)
  between operations  0.69 us (1%)
    pallas_call x1, Pallas kernels, build_table(): pl.pallas_call(functools.partial(exchange_kernel, patch_rows, patch_cols,...  24.4 us
    pallas_call x1, Pallas kernels, compute(): pl.pallas_call(functools.partial(compute_kernel, group, block_len, tile_n...  17.9 us
    unnamed x4, local copies, waits for them, and re-layouts  2.05 us
    select_n x1, other arithmetic, per_device(): jnp.where(sender < 0, -1, jnp.where(is_near, near_index, far_index))  1.35 us
    dot_general x1, matrix products, dot(): return jnp.dot(a, b, preferred_element_type=F32)  1.33 us

profile of v2, /device:TPU:0, one launch (start us, length us, event | category | flops | bytes accessed | tf_op | source)
XLA Modules:
  0.0 47.8 jit_solution(165974532673166263)
XLA Ops:
  0.7 1.3 %fusion.15 = s32[2048]{0:T(1024)} fusion(s32[2048]{0:T(1024)} %param.13, s32[]{:T(128)S(6)} %mul.36, s32[]{:T(128)S(6)} %mul.35), kind=kLoop, calls=%fused_computation.45 | loop fusion | flops 278528 | bytes 16392 | tf_op jit(solution)/shard_map/jit(_where)/select_n | solution.py:210
  2.0 1.3 %convolution_convert_fusion.picked_ref = bf16[64,512]{1,0:T(8,128)(2,1)S(1)} fusion(bf16[512,512]{1,0:T(8,128)(2,1)} %bitcast.7, s32[64]{0:T(128)S(1)} %get-tuple-element.13, s32[64]{0:T(128)S(1)} %get-tuple-element.12, s32[64]{0:T(128)S(1)} %get-tuple-element.9, s32[64]{0:T(128)S(1)} %get-tuple-element.14, s32[64]{0:T(128)S(1)} %get-tuple-element.8, ...), kind=kOutput, calls=%fused_computation | convolution fusion | flops 33849344 | bytes 591616 | tf_op jit(solution)/shard_map/dot_general | solution.py:16
  3.4 0.0 copy-start.1
  3.4 1.0 %copy-done.1 = bf16[16,32,512]{2,1,0:T(8,128)(2,1)S(1)} copy-done((bf16[16,32,512]{2,1,0:T(8,128)(2,1)S(1)}, bf16[16,32,512]{2,1,0:T(8,128)(2,1)}, u32[]{:S(2)}) %copy-start.1) | copy-done | bytes 524312
  4.4 24.4 %shard_map.122.table_ref = bf16[1152,512]{1,0:T(8,128)(2,1)S(1)} custom-call(bf16[512,512]{1,0:T(8,128)(2,1)S(1)} %bitcast.9, bf16[64,512]{1,0:T(8,128)(2,1)S(1)} %convolution_convert_fusion.picked_ref), custom_call_target="tpu_custom_call" | custom-call | tf_op jit(solution)/shard_map/pallas_call | solution.py:366
  28.8 0.0 copy-start
  28.9 1.0 %copy-done = bf16[1152,512]{1,0:T(8,128)(2,1)} copy-done((bf16[1152,512]{1,0:T(8,128)(2,1)}, bf16[1152,512]{1,0:T(8,128)(2,1)S(1)}, u32[]{:S(2)}) %copy-start) | copy-done | bytes 1179672
  29.9 17.9 %shard_map.123 = (bf16[512,512]{1,0:T(8,128)(2,1)}, bf16[2048,512]{1,0:T(8,128)(2,1)}) custom-call(s32[16]{0:T(128)} %tile_ref.1, bf16[2048,512]{1,0:T(8,128)(2,1)} %edge_ref.1, s32[16,1,128]{2,1,0:T(1,128)} %bitcast.10, s32[16,1,128]{2,1,0:T(1,128)} %bitcast.11, bf16[1152,512]{1,0:T(8,128)(2,1)} %copy-done, bf16[512,512]{1,0:T(8,128)(2,1)} %bitcast.8, ...), custom_call_target="tpu_custom_call" | custom-call | tf_op jit(solution)/shard_map/pallas_call | solution.py:126
  (5 shorter events, 0.0 us)
Async XLA Ops:
  3.4 1.1 %copy-start.1 = (bf16[16,32,512]{2,1,0:T(8,128)(2,1)S(1)}, bf16[16,32,512]{2,1,0:T(8,128)(2,1)}, u32[]{:S(2)}) copy-start(bf16[16,32,512]{2,1,0:T(8,128)(2,1)} %param.11) | copy-start | bytes 1572868
  28.8 1.0 %copy-start = (bf16[1152,512]{1,0:T(8,128)(2,1)}, bf16[1152,512]{1,0:T(8,128)(2,1)S(1)}, u32[]{:S(2)}) copy-start(bf16[1152,512]{1,0:T(8,128)(2,1)S(1)} %shard_map.122.table_ref) | copy-start | bytes 3538948

commit v3 on v2

--- a/solution.py
+++ b/solution.py
@@ -137,7 +137,7 @@
             jax.ShapeDtypeStruct((edge_count, features), BF16),
         ],
         compiler_params=pltpu.CompilerParams(
-            dimension_semantics=("arbitrary",), vmem_limit_bytes=56 * 1024 * 1024
+            dimension_semantics=("arbitrary",), vmem_limit_bytes=50 * 1024 * 1024
         ),
     )(
         block_tile,
@@ -370,7 +370,10 @@
         out_shape=jax.ShapeDtypeStruct((table_len - offset, own.shape[1]), BF16),
         scratch_shapes=sems + [pltpu.SemaphoreType.DMA],
         compiler_params=pltpu.CompilerParams(
-            has_side_effects=True, vmem_limit_bytes=24 * 1024 * 1024
+            has_side_effects=True, vmem_limit_bytes=16 * 1024 * 1024
+        ),
+        cost_estimate=pl.CostEstimate(
+            flops=0, bytes_accessed=40 * chips * own.size // 16, transcendentals=0
         ),
     )(own, picked)
 

time: 48 us -> 46.3 us (0.965)
  Pallas kernels: 42.3 us -> 41 us
  other arithmetic: 1.38 us -> 0.85 us
    pallas_call x1, Pallas kernels: 17.9 us -> 16.6 us  [compute(): pl.pallas_call(functools.partial(compute_kernel, group, block_len, tile_n...]
    select_n x1, other arithmetic: 1.35 us -> 0.82 us  [per_device(): jnp.where(sender < 0, -1, jnp.where(is_near, near_index, far_index))]
    unnamed x4 -> x18, local copies, waits for them, and re-layouts: 2.05 us -> 2.11 us
where the time goes in v3:
time: 46.3 us; the launch traced here: 46 us
  Pallas kernels  41 us (89%)
  local copies, waits for them, and re-layouts  2.11 us (5%)
  matrix products  1.33 us (3%)
  other arithmetic  0.85 us (2%)
  between operations  0.79 us (2%)
    pallas_call x1, Pallas kernels, build_table(): pl.pallas_call(functools.partial(exchange_kernel, patch_rows, patch_cols,...  24.4 us
    pallas_call x1, Pallas kernels, compute(): pl.pallas_call(functools.partial(compute_kernel, group, block_len, tile_n...  16.6 us
    unnamed x18, local copies, waits for them, and re-layouts  2.11 us
    dot_general x1, matrix products, dot(): return jnp.dot(a, b, preferred_element_type=F32)  1.33 us

profile of v3, /device:TPU:0, one launch (start us, length us, event | category | flops | bytes accessed | tf_op | source)
XLA Modules:
  0.0 46.0 jit_solution(3187665518667449898)
XLA Ops:
  0.6 0.0 copy-start.7
  0.6 0.0 copy-start.6
  0.7 0.0 copy-start.8
  0.7 0.0 copy-start.5
  0.7 0.0 copy-start.1
  0.7 0.8 %fusion.15 = s32[2048]{0:T(1024)S(1)} fusion(s32[2048]{0:T(1024)} %param.13, s32[]{:T(128)S(6)} %mul.36, s32[]{:T(128)S(6)} %mul.35), kind=kLoop, calls=%fused_computation.45 | loop fusion | flops 278528 | bytes 16392 | tf_op jit(solution)/shard_map/jit(_where)/select_n | solution.py:210
  1.6 1.3 %convolution_convert_fusion.picked_ref = bf16[64,512]{1,0:T(8,128)(2,1)S(1)} fusion(bf16[512,512]{1,0:T(8,128)(2,1)} %bitcast.7, s32[64]{0:T(128)S(1)} %get-tuple-element.13, s32[64]{0:T(128)S(1)} %get-tuple-element.12, s32[64]{0:T(128)S(1)} %get-tuple-element.9, s32[64]{0:T(128)S(1)} %get-tuple-element.14, s32[64]{0:T(128)S(1)} %get-tuple-element.8, ...), kind=kOutput, calls=%fused_computation | convolution fusion | flops 33849344 | bytes 591616 | tf_op jit(solution)/shard_map/dot_general | solution.py:16
  2.9 0.0 copy-start
  2.9 1.0 %copy-done = bf16[16,32,512]{2,1,0:T(8,128)(2,1)S(1)} copy-done((bf16[16,32,512]{2,1,0:T(8,128)(2,1)S(1)}, bf16[16,32,512]{2,1,0:T(8,128)(2,1)}, u32[]{:S(2)}) %copy-start) | copy-done | bytes 524312
  4.0 0.0 copy-start.2
  4.0 0.0 copy-start.3
  4.0 24.4 %shard_map.122.table_ref = bf16[1152,512]{1,0:T(8,128)(2,1)S(1)} custom-call(bf16[512,512]{1,0:T(8,128)(2,1)S(1)} %bitcast.8, bf16[64,512]{1,0:T(8,128)(2,1)S(1)} %convolution_convert_fusion.picked_ref), custom_call_target="tpu_custom_call" | custom-call | bytes 20971520 | tf_op jit(solution)/shard_map/pallas_call | solution.py:366
  28.4 0.0 copy-done.7
  28.4 0.0 copy-done.6
  28.4 0.0 copy-done.8
  28.4 0.0 copy-done.5
  28.4 0.0 copy-done.1
  28.4 0.0 copy-done.2
  28.4 0.0 copy-done.3
  28.4 0.0 copy-start.4
  28.5 1.0 %copy-done.4 = bf16[512,512]{1,0:T(8,128)(2,1)S(1)} copy-done((bf16[512,512]{1,0:T(8,128)(2,1)S(1)}, bf16[512,512]{1,0:T(8,128)(2,1)}, u32[]{:S(2)}) %copy-start.4) | copy-done | bytes 524312
  29.5 16.6 %shard_map.123 = (bf16[512,512]{1,0:T(8,128)(2,1)}, bf16[2048,512]{1,0:T(8,128)(2,1)}) custom-call(s32[16]{0:T(128)S(1)} %copy-done.8, bf16[2048,512]{1,0:T(8,128)(2,1)} %edge_ref.1, s32[16,1,128]{2,1,0:T(1,128)S(1)} %bitcast.10, s32[16,1,128]{2,1,0:T(1,128)S(1)} %bitcast.11, bf16[1152,512]{1,0:T(8,128)(2,1)S(1)} %shard_map.122.table_ref, ...), custom_call_target="tpu_custom_call" | custom-call | tf_op jit(solution)/shard_map/pallas_call | solution.py:126
  (5 shorter events, 0.0 us)
Async XLA Ops:
  0.6 27.7 %copy-start.7 = (f32[512]{0:T(512)S(1)}, f32[512]{0:T(512)}, u32[]{:S(2)}) copy-start(f32[512]{0:T(512)} %param.21) | copy-start | bytes 6148
  0.6 27.7 %copy-start.6 = (f32[512]{0:T(512)S(1)}, f32[512]{0:T(512)}, u32[]{:S(2)}) copy-start(f32[512]{0:T(512)} %param.18) | copy-start | bytes 6148
  0.7 27.7 %copy-start.8 = (s32[16]{0:T(128)S(1)}, s32[16]{0:T(128)}, u32[]{:S(2)}) copy-start(s32[16]{0:T(128)} %tile_ref.1) | copy-start | bytes 196
  0.7 27.7 %copy-start.5 = (s32[2048]{0:T(1024)S(1)}, s32[2048]{0:T(1024)}, u32[]{:S(2)}) copy-start(s32[2048]{0:T(1024)} %param.14) | copy-start | bytes 24580
  0.7 27.7 %copy-start.1 = (bf16[16,32,512]{2,1,0:T(8,128)(2,1)S(1)}, bf16[16,32,512]{2,1,0:T(8,128)(2,1)}, u32[]{:S(2)}) copy-start(bf16[16,32,512]{2,1,0:T(8,128)(2,1)} %param.11) | copy-start | bytes 1572868
  2.9 1.1 %copy-start = (bf16[16,32,512]{2,1,0:T(8,128)(2,1)S(1)}, bf16[16,32,512]{2,1,0:T(8,128)(2,1)}, u32[]{:S(2)}) copy-start(bf16[16,32,512]{2,1,0:T(8,128)(2,1)} %param.11) | copy-start | bytes 1572868
  4.0 24.5 %copy-start.2 = (bf16[1024,512]{1,0:T(8,128)(2,1)S(1)}, bf16[1024,512]{1,0:T(8,128)(2,1)}, u32[]{:S(2)}) copy-start(bf16[1024,512]{1,0:T(8,128)(2,1)} %w_node_first_ref.1) | copy-start | bytes 3145732
  4.0 24.5 %copy-start.3 = (bf16[512,512]{1,0:T(8,128)(2,1)S(1)}, bf16[512,512]{1,0:T(8,128)(2,1)}, u32[]{:S(2)}) copy-start(bf16[512,512]{1,0:T(8,128)(2,1)} %w_second_ref.1) | copy-start | bytes 1572868
  28.4 1.0 %copy-start.4 = (bf16[512,512]{1,0:T(8,128)(2,1)S(1)}, bf16[512,512]{1,0:T(8,128)(2,1)}, u32[]{:S(2)}) copy-start(bf16[512,512]{1,0:T(8,128)(2,1)} %w_node_second_ref.1) | copy-start | bytes 1572868
